TPU v7x, 512 devices: a whole 4x8x8 slice. The times are simulated.
512 devices in a mesh: chain: 32 (over x_hi, z, core), term: 16 (over y, x_lo).
Axes of the slice: x: 4 (x_hi: 2, x_lo: 2; x = x_hi * 2 + x_lo), y: 8, z: 8, core: 2. Of those that a mesh axis runs over, the one named last changes fastest.
Arguments:
- wavefunction: bfloat16 [32, 4, 256, 256], P('chain')
- left_ops: bfloat16 [32, 128, 256, 256], P('chain', 'term')
- right_ops: bfloat16 [32, 128, 256, 256], P('chain', 'term')
- term_table: int32 [4, 32, 512], P(None, 'chain', 'term'), may hold values from 0 to 7, as said below
- coefficients: float32 [32, 512], P('chain', 'term'), may hold values from -0.1 to 0.3
- term_counts: int32 [32, 16], P('chain', 'term'), may hold values from 1 to 32, as said below
Outputs:
- first_hamiltonian_image: bfloat16 [32, 4, 256, 256], P('chain', None, 'term')
- second_image: bfloat16 [32, 4, 256, 256], P('chain', None, 'term')
Inputs may be any that keep to these rules, and one draw needn't show every extreme that they name: `term_table`: row 0 and 1 (source and target block) lie in 0 to 3, rows 2 and 3 (operator indices) in 0 to 7. `term_counts`: in every bond at least one term device has all 32 slots live.
All inputs are finite; a program needn't handle non-finite values.
Results may differ from a plain program's by a relative error of at most 0.014.
Values may be sent and summed in bfloat16 or wider, within the bound.
No kernel may reach another device: no remote copies, remote signals or barrier semaphores. Data moves between devices by JAX's collectives and lax.ppermute only.
A program may use at most 64 MiB of HBM per device.

v0:
```python
import jax
import jax.numpy as jnp
from jax import lax
from jax.sharding import PartitionSpec as P

epsilon = 1e-06


def shifted(value, axis, steps):
    count = lax.axis_size(axis)
    pairs = [(source, (source + steps) % count) for source in range(count)]
    return lax.ppermute(value, axis, pairs)


def apply_terms(blocks, left_blocks, right_blocks, term_rows, coef_rows, live_count):
    block_count = blocks.shape[0]
    slot_count = term_rows.shape[1]
    source = term_rows[0]
    target = term_rows[1]
    left_selection = left_blocks[term_rows[2]]
    right_selection = right_blocks[term_rows[3]]
    selected_blocks = blocks[source]
    inner_contraction = jnp.einsum(
        "skh,shu->sku", left_selection, selected_blocks, preferred_element_type=jnp.float32
    ).astype(jnp.bfloat16)
    outer_contraction = jnp.einsum(
        "lbe,leu->lbu", inner_contraction, right_selection, preferred_element_type=jnp.float32
    )
    live_mask = jnp.arange(slot_count, dtype=jnp.int32) < live_count
    weights = jnp.where(live_mask, coef_rows, jnp.float32(0.0))
    routing = (target[None, :] == jnp.arange(block_count, dtype=jnp.int32)[:, None]).astype(
        jnp.float32
    ) * weights[None, :]
    return jnp.einsum("kt,tad->kad", routing, outer_contraction, precision=lax.Precision.HIGHEST)


def body(wavefunction, left_ops, right_ops, term_table, coefficients, term_counts):
    blocks = wavefunction[0]
    neighbour = shifted(right_ops, "chain", -1)
    term_rows = term_table[:, 0, :]
    coef_rows = coefficients[0]
    live_count = term_counts[0, 0]
    left_blocks = left_ops[0]
    right_blocks = neighbour[0]
    first_part = apply_terms(blocks, left_blocks, right_blocks, term_rows, coef_rows, live_count)
    term_parts = lax.axis_size("term")
    row_count = blocks.shape[1] // term_parts
    starting_row = lax.axis_index("term") * row_count
    entry_count = float(blocks.shape[0] * blocks.shape[1] * blocks.shape[2])
    wave_f32 = blocks.astype(jnp.float32)
    wave_norm = jnp.sum(wave_f32 * wave_f32) / entry_count + epsilon
    first = lax.psum(first_part, "term")
    rayleigh = jnp.sum(wave_f32 * first) / entry_count / wave_norm
    residual = first - rayleigh * wave_f32
    direction = (residual * lax.rsqrt(jnp.sum(residual * residual) / entry_count + epsilon)).astype(
        jnp.bfloat16
    )
    second_part = apply_terms(
        direction, left_blocks, right_blocks, term_rows, coef_rows, live_count
    )
    second = lax.psum(second_part.astype(jnp.bfloat16), "term").astype(jnp.float32)
    first_rows = lax.dynamic_slice_in_dim(first, starting_row, row_count, 1)
    second_rows = lax.dynamic_slice_in_dim(second, starting_row, row_count, 1)
    return (first_rows[None].astype(jnp.bfloat16), second_rows[None].astype(jnp.bfloat16))


def solution(mesh):
    in_specs = (
        P("chain", None, None, None),
        P("chain", "term", None, None),
        P("chain", "term", None, None),
        P(None, "chain", "term"),
        P("chain", "term"),
        P("chain", "term"),
    )
    out_specs = (P("chain", None, "term", None), P("chain", None, "term", None))
    return jax.shard_map(body, mesh=mesh, in_specs=in_specs, out_specs=out_specs, check_vma=False)
```

profile of v0, /device:TPU:2, one launch (start us, length us, event | category | flops | bytes accessed | tf_op | source)
XLA Modules:
  0.0 389.5 jit_solution(7426124249693122728)
XLA Ops:
  7.2 0.0 copy-start
  7.2 0.0 all-reduce.3.cloned.1.call-start
  7.2 12.1 %collective-permute-start = (bf16[1,8,256,256]{3,2,1,0:T(8,128)(2,1)}, bf16[1,8,256,256]{3,2,1,0:T(8,128)(2,1)S(1)}, u32[]{:S(2)}, u32[]{:S(2)}) collective-permute-start(bf16[1,8,256,256]{3,2,1,0:T(8,128)(2,1)} %param.8), channel_id=1, source_target_pairs={{0,496},{16,0},{32,16},{48,32},{64,48},{80,64},{96,80},{112,96},{1... | collective-permute-start | bytes 3145736 | tf_op jit(solution)/shard_map/ppermute | solution.py:12
  20.0 1.5 copy.33
  21.4 0.1 copy.12
  21.5 0.7 fusion.32
  22.2 2.7 gather_fusion.1
  24.9 0.0 copy-done
  24.9 0.0 copy-start.2
  25.0 2.8 gather_fusion
  27.7 0.7 slice_bitcast_fusion
  28.4 0.0 copy-done.2
  28.4 3.5 collective-permute-done
  31.9 2.8 gather_fusion.2
  34.7 10.2 %fusion.6 = f32[32,256,256]{2,1,0:T(8,128)} fusion(bf16[32,256,256]{2,1,0:T(8,128)(2,1)} %gather_fusion.2, bf16[32,256,256]{2,1,0:T(8,128)(2,1)} %gather_fusion, bf16[32,256,256]{2,1,0:T(8,128)(2,1)} %gather_fusion.1), kind=kOutput, calls=%fused_computation.10 | convolution fusion | flops 2149580800 | bytes 20971520 | tf_op jit(solution)/shard_map/lbe,leu->lbu/dot_general | solution.py:26
  45.0 0.0 copy-start.1
  45.0 13.2 %fusion.2 = f32[4,256,256]{2,0,1:T(4,128)} fusion(f32[32,256,256]{2,1,0:T(8,128)} %fusion.6, f32[32]{0:T(128)S(1)} %fusion.30, s32[32]{0:T(128)S(1)} %slice_bitcast_fusion), kind=kOutput, calls=%fused_computation.6 | convolution fusion | flops 100663552 | bytes 9437440 | tf_op jit(solution)/shard_map/kt,tad->kad/dot_general | solution.py:34
  58.1 0.0 all-reduce.3.cloned.1.call-update
  58.2 0.2 all-reduce.5.cloned.1.call-start
  58.4 144.4 %all-reduce.3.cloned.1.call-done = f32[4,256,256]{2,0,1:T(4,128)} async-done(((f32[4,256,256]{2,0,1:T(4,128)}), f32[4,256,256]{2,0,1:T(4,128)}) %all-reduce.3.cloned.1.call-update) | async-done | bytes 1048592 | tf_op jit(solution)/shard_map/psum | solution.py:52
  202.8 0.0 copy-done.1
  202.8 2.4 fusion.16
  206.6 2.4 multiply_reduce_fusion
  209.6 1.7 multiply_convert_fusion
  211.4 0.1 copy.13
  211.4 2.7 gather_fusion.3
  214.2 10.2 %fusion.4 = f32[32,256,256]{2,1,0:T(8,128)} fusion(bf16[32,256,256]{2,1,0:T(8,128)(2,1)} %gather_fusion.2, bf16[32,256,256]{2,1,0:T(8,128)(2,1)} %gather_fusion, bf16[32,256,256]{2,1,0:T(8,128)(2,1)} %gather_fusion.3), kind=kOutput, calls=%fused_computation.8 | convolution fusion | flops 2149580800 | bytes 20971520 | tf_op jit(solution)/shard_map/lbe,leu->lbu/dot_general | solution.py:26
  224.4 13.0 %fusion.12 = bf16[4,256,256]{2,0,1:T(4,128)(2,1)} fusion(f32[32,256,256]{2,1,0:T(8,128)} %fusion.4, f32[32]{0:T(128)S(1)} %fusion.30, s32[32]{0:T(128)S(1)} %slice_bitcast_fusion), kind=kOutput, calls=%fused_computation.17 | convolution fusion | flops 100925696 | bytes 8913152 | tf_op jit(solution)/shard_map/kt,tad->kad/dot_general | solution.py:34
  237.4 0.0 all-reduce.5.cloned.1.call-update
  237.4 0.9 fusion.18
  238.3 0.6 copy.14
  238.9 142.4 %all-reduce.5.cloned.1.call-done = bf16[4,256,256]{2,0,1:T(4,128)(2,1)} async-done(((bf16[4,256,256]{2,0,1:T(4,128)(2,1)}), bf16[4,256,256]{2,0,1:T(4,128)(2,1)}) %all-reduce.5.cloned.1.call-update) | async-done | bytes 524304 | tf_op jit(solution)/shard_map/psum | solution.py:61
  381.3 0.8 fusion.19
  382.1 0.6 copy.15
  (3 shorter events, 0.0 us)
Async XLA Ops:
  7.2 17.8 %copy-start = (bf16[1,8,256,256]{3,2,1,0:T(8,128)(2,1)S(1)}, bf16[1,8,256,256]{3,2,1,0:T(8,128)(2,1)}, u32[]{:S(2)}) copy-start(bf16[1,8,256,256]{3,2,1,0:T(8,128)(2,1)} %param.7) | copy-start | bytes 3145732
  7.2 195.6 %all-reduce.3.cloned.1.call-start = ((), (), s32[]{:S(2)}) async-start(), calls=%async_computation | async-start | bytes 2097152 | tf_op jit(solution)/shard_map/psum | solution.py:52
  7.2 24.7 %collective-permute-start = (bf16[1,8,256,256]{3,2,1,0:T(8,128)(2,1)}, bf16[1,8,256,256]{3,2,1,0:T(8,128)(2,1)S(1)}, u32[]{:S(2)}, u32[]{:S(2)}) collective-permute-start(bf16[1,8,256,256]{3,2,1,0:T(8,128)(2,1)} %param.8), channel_id=1, source_target_pairs={{0,496},{16,0},{32,16},{48,32},{64,48},{80,64},{96,80},{112,96},{1... | collective-permute-start | bytes 3145736 | tf_op jit(solution)/shard_map/ppermute | solution.py:12
  24.9 3.4 copy-start.2
  45.0 157.9 %copy-start.1 = (bf16[1,4,256,256]{3,2,1,0:T(8,128)(2,1)S(1)}, bf16[1,4,256,256]{3,2,1,0:T(8,128)(2,1)}, u32[]{:S(2)}) copy-start(bf16[1,4,256,256]{3,2,1,0:T(8,128)(2,1)} %param.6) | copy-start | bytes 1572868
  58.2 323.1 %all-reduce.5.cloned.1.call-start = ((), (), s32[]{:S(2)}) async-start(), calls=%async_computation.1 | async-start | bytes 1048576 | tf_op jit(solution)/shard_map/psum | solution.py:61
Sparse Core Ops, SparseCore 0:
  58.3 144.4 all-reduce.2
  237.6 143.6 all-reduce.4
where the time goes:
time: 390 us
  waiting for transfers between devices  290 us (74%)
  matrix products  46.7 us (12%)
  between operations  16.8 us (4%)
  local copies, waits for them, and re-layouts  15.4 us (4%)
  starting transfers between devices  12.3 us (3%)
  other arithmetic  7.98 us (2%)
    psum x1, waiting for transfers between devices, body(): first = lax.psum(first_part, 'term')  144 us
    psum x1, waiting for transfers between devices, body(): lax.psum(second_part.astype(jnp.bfloat16), 'term').astype(jnp.float32)  142 us
    dot_general x2, matrix products, apply_terms(): jnp.einsum('kt,tad->kad', routing, outer_contraction, precision=lax.Preci...  26.2 us
    dot_general x2, matrix products, apply_terms(): jnp.einsum('lbe,leu->lbu', inner_contraction, right_selection, preferred_...  20.5 us
    ppermute x1, starting transfers between devices, shifted(): return lax.ppermute(value, axis, pairs)  12.1 us
  transfers between devices with their start and end apart: 3, of which 3 were waited for; matrix products, arithmetic and copies ran while one was open for 3% of the time, Pallas kernels for 0%

commit v1 on v0

v1 whole, which is shorter than its diff:
```python
import jax
import jax.numpy as jnp
from jax import lax
from jax.experimental import pallas as pl
from jax.experimental.pallas import tpu as pltpu
from jax.sharding import PartitionSpec as P

epsilon = 1e-06
VMEM = pl.BlockSpec(memory_space=pltpu.VMEM)
SMEM = pl.BlockSpec(memory_space=pltpu.SMEM)
F32 = jnp.float32
BF16 = jnp.bfloat16
EXTRA = 8


def left_products(left_ref, vector, product_ref):
    def step(li, _):
        left = left_ref[0, li]
        for src in range(4):
            product_ref[src, li] = jnp.dot(left, vector(src), preferred_element_type=F32).astype(BF16)
        return 0

    lax.fori_loop(0, 8, step, 0)


def right_sums(table_ref, coef_ref, count_ref, product_ref, right_ref, total_ref):
    total_ref[...] = jnp.zeros_like(total_ref)
    count = count_ref[0, 0]

    def step(slot, _):
        weight = jnp.where(slot < count, coef_ref[0, slot], F32(0.0))
        inner = product_ref[table_ref[0, 0, slot], table_ref[2, 0, slot]]
        outer = jnp.dot(inner, right_ref[0, table_ref[3, 0, slot]], preferred_element_type=F32)
        dst = table_ref[1, 0, slot]
        total_ref[dst] = total_ref[dst] + weight * outer
        return 0

    lax.fori_loop(0, 32, step, 0, unroll=2)


def first_left_kernel(left_ref, wave_ref, product_ref, norm_ref):
    left_products(left_ref, lambda src: wave_ref[0, src], product_ref)
    norm = F32(0.0)
    for k in range(4):
        x = wave_ref[0, k].astype(F32)
        norm = norm + jnp.sum(x * x)
    norm_ref[0, 0] = norm


def first_right_kernel(order, table_ref, coef_ref, count_ref, product_ref, right_ref, wave_ref, out_ref, total_ref):
    right_sums(table_ref, coef_ref, count_ref, product_ref, right_ref, total_ref)
    share = F32(0.0)
    for k in range(4):
        share = share + jnp.sum(wave_ref[0, k].astype(F32) * total_ref[k])
        for place, owner in enumerate(order):
            out_ref[place, pl.ds(16 * k, 16), :] = total_ref[k, pl.ds(16 * owner, 16), :].astype(BF16)
    whole = jnp.full((EXTRA, 256), share, F32)
    high = whole.astype(BF16).astype(F32)
    middle = (whole - high).astype(BF16).astype(F32)
    low = whole - high - middle
    row = lax.broadcasted_iota(jnp.int32, (EXTRA, 256), 0)
    pieces = jnp.where(row == 0, high, jnp.where(row == 1, middle, jnp.where(row == 2, low, 0.0))).astype(BF16)
    for place in range(len(order)):
        out_ref[place, pl.ds(64, EXTRA), :] = pieces


def residual_kernel(place_ref, norm_ref, parts_ref, wave_ref, first_ref, copies_ref):
    entries = 4 * 256 * 256
    rows = parts_ref[0].astype(F32)
    for part in range(1, 16):
        rows = rows + parts_ref[part].astype(F32)
    overlap = jnp.sum(rows[64:, 0:1])
    first = rows[:64]
    first_ref[0] = first.reshape(4, 16, 256).astype(BF16)
    rayleigh = overlap / entries / (norm_ref[0, 0] / entries + epsilon)
    start = pl.multiple_of(place_ref[0, 0] * 16, 16)
    wave = wave_ref[0, :, pl.ds(start, 16), :].astype(F32).reshape(64, 256)
    residual = (first - rayleigh * wave).astype(BF16)
    for copy in range(16):
        copies_ref[copy] = residual


def second_kernel(
    order, table_ref, coef_ref, count_ref, blocks_ref, left_ref, right_ref, out_ref, scale_ref, vector_ref, product_ref, total_ref
):
    entries = 4 * 256 * 256
    for place, owner in enumerate(order):
        for k in range(4):
            vector_ref[k, pl.ds(16 * owner, 16), :] = blocks_ref[place, pl.ds(16 * k, 16), :]
    left_products(left_ref, lambda src: vector_ref[src], product_ref)
    right_sums(table_ref, coef_ref, count_ref, product_ref, right_ref, total_ref)
    for k in range(4):
        for place, owner in enumerate(order):
            out_ref[place, pl.ds(16 * k, 16), :] = total_ref[k, pl.ds(16 * owner, 16), :].astype(BF16)
    square = F32(0.0)
    for k in range(4):
        r = vector_ref[k].astype(F32)
        square = square + jnp.sum(r * r)
    scale_ref[...] = lax.rsqrt(jnp.full((1, 128), square / entries + epsilon, F32))


def scale_kernel(scale_ref, parts_ref, out_ref):
    rows = parts_ref[0].astype(F32)
    for part in range(1, 16):
        rows = rows + parts_ref[part].astype(F32)
    scale = jnp.concatenate([scale_ref[...], scale_ref[...]], axis=1)
    out_ref[0] = (rows * scale).reshape(4, 16, 256).astype(BF16)


def params(mib):
    return pltpu.CompilerParams(vmem_limit_bytes=mib << 20)


ORDER = (0, 2, 4, 6, 8, 10, 12, 14, 15, 13, 11, 9, 7, 5, 3, 1)


def exchange(blocks):
    return lax.all_to_all(blocks, "term", 0, 0, axis_index_groups=[list(ORDER)])


def body(wavefunction, left_ops, right_ops, term_table, coefficients, term_counts):
    import functools

    count = lax.axis_size("chain")
    right = lax.ppermute(right_ops, "chain", [(s, (s - 1) % count) for s in range(count)])
    place = lax.axis_index("term").reshape(1, 1).astype(jnp.int32)
    shape = jax.ShapeDtypeStruct
    product, norm = pl.pallas_call(
        first_left_kernel,
        out_shape=(shape((4, 8, 256, 256), BF16), shape((1, 1), F32)),
        in_specs=[VMEM, VMEM],
        out_specs=(VMEM, SMEM),
        compiler_params=params(12),
        name="first_left",
    )(left_ops, wavefunction)
    partial = pl.pallas_call(
        functools.partial(first_right_kernel, ORDER),
        out_shape=shape((16, 64 + EXTRA, 256), BF16),
        in_specs=[SMEM, SMEM, SMEM, VMEM, VMEM, VMEM],
        out_specs=VMEM,
        scratch_shapes=[pltpu.VMEM((4, 256, 256), F32)],
        compiler_params=params(16),
        name="first_right",
    )(term_table, coefficients, term_counts, product, right, wavefunction)
    first, copies = pl.pallas_call(
        residual_kernel,
        out_shape=(shape((1, 4, 16, 256), BF16), shape((16, 64, 256), BF16)),
        in_specs=[SMEM, SMEM, VMEM, VMEM],
        out_specs=(VMEM, VMEM),
        compiler_params=params(8),
        name="residual",
    )(place, norm, exchange(partial), wavefunction)
    partial, scale = pl.pallas_call(
        functools.partial(second_kernel, ORDER),
        out_shape=(shape((16, 64, 256), BF16), shape((1, 128), F32)),
        in_specs=[SMEM, SMEM, SMEM, VMEM, VMEM, VMEM],
        out_specs=(VMEM, VMEM),
        scratch_shapes=[
            pltpu.VMEM((4, 256, 256), BF16),
            pltpu.VMEM((4, 8, 256, 256), BF16),
            pltpu.VMEM((4, 256, 256), F32),
        ],
        compiler_params=params(16),
        name="second",
    )(term_table, coefficients, term_counts, exchange(copies), left_ops, right)
    second = pl.pallas_call(
        scale_kernel,
        out_shape=shape((1, 4, 16, 256), BF16),
        in_specs=[VMEM, VMEM],
        out_specs=VMEM,
        compiler_params=params(8),
        name="scale",
    )(scale, exchange(partial))
    return first, second


def solution(mesh):
    in_specs = (
        P("chain", None, None, None),
        P("chain", "term", None, None),
        P("chain", "term", None, None),
        P(None, "chain", "term"),
        P("chain", "term"),
        P("chain", "term"),
    )
    out_specs = (P("chain", None, "term", None), P("chain", None, "term", None))
    return jax.shard_map(body, mesh=mesh, in_specs=in_specs, out_specs=out_specs, check_vma=False)
```

time: 390 us -> 101 us (0.26)
  the two profiles are of different devices: /device:TPU:2 before, /device:TPU:326 now
where the time goes in v1:
time: 101 us
  blocking collectives  40.8 us (40%)
  waiting for transfers between devices  25.2 us (25%)
  Pallas kernels  18.5 us (18%)
  starting transfers between devices  10.5 us (10%)
  local copies, waits for them, and re-layouts  4.65 us (5%)
  between operations  1.32 us (1%)
    all_to_all x2, blocking collectives, exchange(): return lax.all_to_all(blocks, 'term', 0, 0, axis_index_groups=[list(ORDER)])  40.8 us
    all_to_all x1, waiting for transfers between devices, exchange(): return lax.all_to_all(blocks, 'term', 0, 0, axis_index_groups=[list(ORDER)])  18.7 us
    all_to_all x1, starting transfers between devices, exchange(): return lax.all_to_all(blocks, 'term', 0, 0, axis_index_groups=[list(ORDER)])  8.58 us
    pallas_call x1, Pallas kernels, body(): pl.pallas_call(functools.partial(second_kernel, ORDER), out_shape=(shape(...  7.47 us
    ppermute x1, waiting for transfers between devices, body(): lax.ppermute(right_ops, 'chain', [(s, (s - 1) % count) for s in range(cou...  6.5 us
    pallas_call x1, Pallas kernels, body(): pl.pallas_call(functools.partial(first_right_kernel, ORDER), out_shape=sh...  5.87 us
    unnamed x18, local copies, waits for them, and re-layouts  4.65 us
    pallas_call x1, Pallas kernels, body(): pl.pallas_call(first_left_kernel, out_shape=(shape((4, 8, 256, 256), BF16...  3.18 us
  transfers between devices with their start and end apart: 2, of which 2 were waited for; matrix products, arithmetic and copies ran while one was open for 0% of the time, Pallas kernels for 3%

profile of v1, /device:TPU:326, one launch (start us, length us, event | category | flops | bytes accessed | tf_op | source)
XLA Modules:
  0.0 100.9 jit_solution(11448153546961389994)
XLA Ops:
  0.6 1.9 %collective-permute-start = (bf16[1,8,256,256]{3,2,1,0:T(8,128)(2,1)}, bf16[1,8,256,256]{3,2,1,0:T(8,128)(2,1)S(1)}, u32[]{:S(2)}, u32[]{:S(2)}) collective-permute-start(bf16[1,8,256,256]{3,2,1,0:T(8,128)(2,1)} %param.8), channel_id=1, source_target_pairs={{0,496},{16,0},{32,16},{48,32},{64,48},{80,64},{96,80},{112,96},{1... | collective-permute-start | bytes 3145736 | tf_op jit(solution)/shard_map/ppermute | solution.py:125
  3.2 0.0 copy-start
  3.2 1.0 %copy-done = bf16[1,4,256,256]{3,2,1,0:T(8,128)(2,1)S(1)} copy-done((bf16[1,4,256,256]{3,2,1,0:T(8,128)(2,1)S(1)}, bf16[1,4,256,256]{3,2,1,0:T(8,128)(2,1)}, u32[]{:S(2)}) %copy-start) | copy-done | bytes 524312
  4.2 0.0 copy-start.3
  4.2 1.2 %copy-done.3 = bf16[1,8,256,256]{3,2,1,0:T(8,128)(2,1)S(1)} copy-done((bf16[1,8,256,256]{3,2,1,0:T(8,128)(2,1)S(1)}, bf16[1,8,256,256]{3,2,1,0:T(8,128)(2,1)}, u32[]{:S(2)}) %copy-start.3) | copy-done | bytes 1048600
  5.5 0.0 copy-start.2
  5.5 3.2 %first_left.1 = (bf16[4,8,256,256]{3,2,1,0:T(8,128)(2,1)S(1)}, f32[1,1]{1,0:T(1,128)}) custom-call(bf16[1,8,256,256]{3,2,1,0:T(8,128)(2,1)S(1)} %copy-done.3, bf16[1,4,256,256]{3,2,1,0:T(8,128)(2,1)S(1)} %copy-done), custom_call_target="tpu_custom_call" | custom-call | tf_op jit(solution)/shard_map/first_left/pallas_call | solution.py:128
  8.7 6.5 %collective-permute-done.right_ref = bf16[1,8,256,256]{3,2,1,0:T(8,128)(2,1)S(1)} collective-permute-done((bf16[1,8,256,256]{3,2,1,0:T(8,128)(2,1)}, bf16[1,8,256,256]{3,2,1,0:T(8,128)(2,1)S(1)}, u32[]{:S(2)}, u32[]{:S(2)}) %collective-permute-start) | collective-permute-done | bytes 1048608 | tf_op jit(solution)/shard_map/ppermute | solution.py:125
  15.2 0.0 copy-start.1
  15.2 1.0 %copy-done.1 = bf16[1,4,256,256]{3,2,1,0:T(8,128)(2,1)S(1)} copy-done((bf16[1,4,256,256]{3,2,1,0:T(8,128)(2,1)S(1)}, bf16[1,4,256,256]{3,2,1,0:T(8,128)(2,1)}, u32[]{:S(2)}) %copy-start.1) | copy-done | bytes 524312
  16.2 0.0 copy-start.5
  16.2 0.7 copy-done.5
  16.9 0.0 copy-start.7
  16.9 0.7 copy-done.7
  17.5 0.0 copy-start.4
  17.6 0.0 copy-start.6
  17.6 0.0 copy-start.8
  17.6 5.9 %first_right.1 = bf16[16,72,256]{2,1,0:T(8,128)(2,1)} custom-call(s32[4,1,32]{2,1,0:T(1,128)S(1)} %copy-done.5, f32[1,32]{1,0:T(1,128)S(1)} %copy-done.7, s32[1,1]{1,0:T(1,128)S(6)} %copy.8.count_ref, bf16[4,8,256,256]{3,2,1,0:T(8,128)(2,1)S(1)} %get-tuple-element.9.product_ref, bf16[1,8,256,256]{3,2,1,0:T(8,128)(2,1)S(1)} %collective-permute-done.right_ref, ...), custom_call_target="tpu_custom_call" | custom-call | tf_op jit(solution)/shard_map/first_right/pallas_call | solution.py:136
  23.4 8.6 %all-to-all-start = ((bf16[16,72,256]{2,1,0:T(8,128)(2,1)}), bf16[16,72,256]{2,1,0:T(8,128)(2,1)S(1)}, u32[]{:S(2)}, u32[]{:S(2)}) async-start(bf16[16,72,256]{2,1,0:T(8,128)(2,1)} %first_right.1), calls=%async_computation | async-start | bytes 1179648 | tf_op jit(solution)/shard_map/all_to_all | solution.py:118
  32.0 18.7 %all-to-all-done.parts_ref = bf16[16,72,256]{2,1,0:T(8,128)(2,1)S(1)} async-done(((bf16[16,72,256]{2,1,0:T(8,128)(2,1)}), bf16[16,72,256]{2,1,0:T(8,128)(2,1)S(1)}, u32[]{:S(2)}, u32[]{:S(2)}) %all-to-all-start) | async-done | bytes 589856 | tf_op jit(solution)/shard_map/all_to_all | solution.py:118
  50.7 0.0 copy-done.2
  50.7 1.3 %residual.1 = (bf16[1,4,16,256]{3,2,1,0:T(8,128)(2,1)}, bf16[16,64,256]{2,1,0:T(8,128)(2,1)S(1)}) custom-call(s32[1,1]{1,0:T(1,128)} %bitcast.place_ref, f32[1,1]{1,0:T(1,128)} %get-tuple-element.8.norm_ref, bf16[16,72,256]{2,1,0:T(8,128)(2,1)S(1)} %all-to-all-done.parts_ref, bf16[1,4,256,256]{3,2,1,0:T(8,128)(2,1)S(1)} %copy-done.2), custom_call_target="tpu_custom_call" | custom-call | tf_op jit(solution)/shard_map/residual/pallas_call | solution.py:145
  52.0 20.8 %all_to_all.15.blocks_ref = bf16[16,64,256]{2,1,0:T(8,128)(2,1)S(1)} all-to-all(bf16[16,64,256]{2,1,0:T(8,128)(2,1)S(1)} %get-tuple-element.11), channel_id=1, replica_groups={{0,2,4,6,8,10,12,14,15,13,11,9,7,5,3,1},{16,18,20,22,24,26,28,30,31,29,..., dimensions={0} | all-to-all | bytes 1048576 | tf_op jit(solution)/shard_map/all_to_all | solution.py:118
  72.8 0.0 copy-done.4
  72.8 0.0 copy-done.6
  72.8 0.0 copy-done.8
  72.8 7.5 %second.1 = (bf16[16,64,256]{2,1,0:T(8,128)(2,1)S(1)}, f32[1,128]{1,0:T(1,128)S(1)}) custom-call(s32[4,1,32]{2,1,0:T(1,128)S(1)} %copy-done.6, f32[1,32]{1,0:T(1,128)S(1)} %copy-done.8, s32[1,1]{1,0:T(1,128)S(6)} %copy.8.count_ref, bf16[16,64,256]{2,1,0:T(8,128)(2,1)S(1)} %all_to_all.15.blocks_ref, bf16[1,8,256,256]{3,2,1,0:T(8,128)(2,1)S(1)} %copy-done.4, ...), custom_call_target="tpu_custom_call" | custom-call | tf_op jit(solution)/shard_map/second/pallas_call | solution.py:153
  80.3 20.0 %all_to_all.16.parts_ref = bf16[16,64,256]{2,1,0:T(8,128)(2,1)S(1)} all-to-all(bf16[16,64,256]{2,1,0:T(8,128)(2,1)S(1)} %get-tuple-element.13), channel_id=1, replica_groups={{0,2,4,6,8,10,12,14,15,13,11,9,7,5,3,1},{16,18,20,22,24,26,28,30,31,29,..., dimensions={0} | all-to-all | bytes 1048576 | tf_op jit(solution)/shard_map/all_to_all | solution.py:118
  100.2 0.7 scale.1
Async XLA Ops:
  0.6 14.5 %collective-permute-start = (bf16[1,8,256,256]{3,2,1,0:T(8,128)(2,1)}, bf16[1,8,256,256]{3,2,1,0:T(8,128)(2,1)S(1)}, u32[]{:S(2)}, u32[]{:S(2)}) collective-permute-start(bf16[1,8,256,256]{3,2,1,0:T(8,128)(2,1)} %param.8), channel_id=1, source_target_pairs={{0,496},{16,0},{32,16},{48,32},{64,48},{80,64},{96,80},{112,96},{1... | collective-permute-start | bytes 3145736 | tf_op jit(solution)/shard_map/ppermute | solution.py:125
  3.2 1.0 %copy-start = (bf16[1,4,256,256]{3,2,1,0:T(8,128)(2,1)S(1)}, bf16[1,4,256,256]{3,2,1,0:T(8,128)(2,1)}, u32[]{:S(2)}) copy-start(bf16[1,4,256,256]{3,2,1,0:T(8,128)(2,1)} %wave_ref.5) | copy-start | bytes 1572868
  4.2 1.2 %copy-start.3 = (bf16[1,8,256,256]{3,2,1,0:T(8,128)(2,1)S(1)}, bf16[1,8,256,256]{3,2,1,0:T(8,128)(2,1)}, u32[]{:S(2)}) copy-start(bf16[1,8,256,256]{3,2,1,0:T(8,128)(2,1)} %left_ref.3) | copy-start | bytes 3145732
  5.5 45.2 %copy-start.2 = (bf16[1,4,256,256]{3,2,1,0:T(8,128)(2,1)S(1)}, bf16[1,4,256,256]{3,2,1,0:T(8,128)(2,1)}, u32[]{:S(2)}) copy-start(bf16[1,4,256,256]{3,2,1,0:T(8,128)(2,1)} %wave_ref.5) | copy-start | bytes 1572868
  15.2 1.0 %copy-start.1 = (bf16[1,4,256,256]{3,2,1,0:T(8,128)(2,1)S(1)}, bf16[1,4,256,256]{3,2,1,0:T(8,128)(2,1)}, u32[]{:S(2)}) copy-start(bf16[1,4,256,256]{3,2,1,0:T(8,128)(2,1)} %wave_ref.5) | copy-start | bytes 1572868
  16.2 0.7 copy-start.5
  16.9 0.7 copy-start.7
  17.5 55.2 %copy-start.4 = (bf16[1,8,256,256]{3,2,1,0:T(8,128)(2,1)S(1)}, bf16[1,8,256,256]{3,2,1,0:T(8,128)(2,1)}, u32[]{:S(2)}) copy-start(bf16[1,8,256,256]{3,2,1,0:T(8,128)(2,1)} %left_ref.3) | copy-start | bytes 3145732
  17.6 55.2 %copy-start.6 = (s32[4,1,32]{2,1,0:T(1,128)S(1)}, s32[4,1,32]{2,1,0:T(1,128)}, u32[]{:S(2)}) copy-start(s32[4,1,32]{2,1,0:T(1,128)} %table_ref.3) | copy-start | bytes 1540
  17.6 55.2 %copy-start.8 = (f32[1,32]{1,0:T(1,128)S(1)}, f32[1,32]{1,0:T(1,128)}, u32[]{:S(2)}) copy-start(f32[1,32]{1,0:T(1,128)} %coef_ref.3) | copy-start | bytes 388
  23.4 27.2 %all-to-all-start = ((bf16[16,72,256]{2,1,0:T(8,128)(2,1)}), bf16[16,72,256]{2,1,0:T(8,128)(2,1)S(1)}, u32[]{:S(2)}, u32[]{:S(2)}) async-start(bf16[16,72,256]{2,1,0:T(8,128)(2,1)} %first_right.1), calls=%async_computation | async-start | bytes 1179648 | tf_op jit(solution)/shard_map/all_to_all | solution.py:118

commit v2 on v1

v2 whole, which is shorter than its diff:
```python
import functools

import jax
import jax.numpy as jnp
from jax import lax
from jax.experimental import pallas as pl
from jax.experimental.pallas import tpu as pltpu
from jax.sharding import PartitionSpec as P

epsilon = 1e-06
VMEM = pl.BlockSpec(memory_space=pltpu.VMEM)
SMEM = pl.BlockSpec(memory_space=pltpu.SMEM)
F32 = jnp.float32
BF16 = jnp.bfloat16
HBM = pl.BlockSpec(memory_space=pltpu.HBM)


def left_products(left_ref, vector, product_ref):
    left = left_ref[0].reshape(8 * 256, 256)
    for src in range(4):
        product = jnp.dot(left, vector(src), preferred_element_type=F32)
        product_ref[src] = product.astype(BF16).reshape(8, 256, 256)


def right_sums(table_ref, coef_ref, count_ref, product_ref, right_ref, total_ref):
    total_ref[...] = jnp.zeros_like(total_ref)
    count = count_ref[0, 0]

    def step(slot, _):
        weight = jnp.where(slot < count, coef_ref[0, slot], F32(0.0))
        inner = product_ref[table_ref[0, 0, slot], table_ref[2, 0, slot]]
        outer = jnp.dot(inner, right_ref[0, table_ref[3, 0, slot]], preferred_element_type=F32)
        dst = table_ref[1, 0, slot]
        total_ref[dst] = total_ref[dst] + weight * outer
        return 0

    lax.fori_loop(0, 32, step, 0, unroll=16)


def stage_kernel(table_ref, coef_ref, left_ref, wave_ref, table_out, coef_out, left_out, wave_out, sems):
    copies = [
        pltpu.make_async_copy(source, target, sems.at[i])
        for i, (source, target) in enumerate(
            ((left_ref, left_out), (wave_ref, wave_out), (table_ref, table_out), (coef_ref, coef_out))
        )
    ]
    for copy in copies:
        copy.start()
    for copy in copies:
        copy.wait()


def first_left_kernel(table_ref, coef_ref, count_ref, left_ref, wave_ref, mixed_ref, norm_ref, sum_ref):
    sum_ref[...] = jnp.zeros_like(sum_ref)
    count = count_ref[0, 0]

    def step(slot, _):
        weight = jnp.where(slot < count, coef_ref[0, slot], F32(0.0))
        inner = jnp.dot(
            left_ref[0, table_ref[2, 0, slot]], wave_ref[0, table_ref[0, 0, slot]], preferred_element_type=F32
        )
        cell = table_ref[1, 0, slot] * 8 + table_ref[3, 0, slot]
        sum_ref[cell] = sum_ref[cell] + weight * inner
        return 0

    lax.fori_loop(0, 32, step, 0, unroll=16)
    norm = F32(0.0)
    for k in range(4):
        x = wave_ref[0, k].astype(F32)
        norm = norm + jnp.sum(x * x)
        for ri in range(8):
            mixed_ref[k, :, pl.ds(256 * ri, 256)] = sum_ref[k * 8 + ri].astype(BF16)
    norm_ref[...] = jnp.full((1, 128), norm, F32)


def first_right_kernel(order, late_ref, mixed_ref, right_ref, out_ref):
    pl.delay(late_ref[0, 0])

    right = right_ref[0].reshape(8 * 256, 256)
    for k in range(4):
        total = jnp.dot(mixed_ref[k], right, preferred_element_type=F32)
        for place, owner in enumerate(order):
            out_ref[place, pl.ds(16 * k, 16), :] = total[16 * owner : 16 * owner + 16].astype(BF16)


def sum_kernel(parts_ref, first_ref, copies_ref):
    rows = parts_ref[0].astype(F32)
    for part in range(1, 16):
        rows = rows + parts_ref[part].astype(F32)
    first = rows.astype(BF16)
    first_ref[0] = first.reshape(4, 16, 256)
    for copy in range(16):
        copies_ref[copy] = first


def second_kernel(
    order,
    table_ref,
    coef_ref,
    count_ref,
    norm_ref,
    blocks_ref,
    wave_ref,
    left_ref,
    right_ref,
    out_ref,
    scale_ref,
    vector_ref,
    product_ref,
    total_ref,
):
    entries = 4 * 256 * 256
    overlap = jnp.zeros((16, 256), F32)
    for place, owner in enumerate(order):
        for k in range(4):
            first = blocks_ref[place, pl.ds(16 * k, 16), :].astype(F32)
            overlap = overlap + first * wave_ref[0, k, pl.ds(16 * owner, 16), :].astype(F32)
    rayleigh = jnp.sum(overlap) / entries / (jnp.max(norm_ref[...]) / entries + epsilon)
    square = jnp.zeros((16, 256), F32)
    for place, owner in enumerate(order):
        for k in range(4):
            first = blocks_ref[place, pl.ds(16 * k, 16), :].astype(F32)
            residual = first - rayleigh * wave_ref[0, k, pl.ds(16 * owner, 16), :].astype(F32)
            square = square + residual * residual
            vector_ref[k, pl.ds(16 * owner, 16), :] = residual.astype(BF16)
    left_products(left_ref, lambda src: vector_ref[src], product_ref)
    right_sums(table_ref, coef_ref, count_ref, product_ref, right_ref, total_ref)
    for k in range(4):
        for place, owner in enumerate(order):
            out_ref[place, pl.ds(16 * k, 16), :] = total_ref[k, pl.ds(16 * owner, 16), :].astype(BF16)
    scale_ref[...] = lax.rsqrt(jnp.full((1, 128), jnp.sum(square) / entries + epsilon, F32))


def scale_kernel(scale_ref, parts_ref, out_ref):
    rows = parts_ref[0].astype(F32)
    for part in range(1, 16):
        rows = rows + parts_ref[part].astype(F32)
    scale = jnp.concatenate([scale_ref[...], scale_ref[...]], axis=1)
    out_ref[0] = (rows * scale).reshape(4, 16, 256).astype(BF16)


def params(mib):
    return pltpu.CompilerParams(vmem_limit_bytes=mib << 20)


ORDER = (0, 2, 4, 6, 8, 10, 12, 14, 15, 13, 11, 9, 7, 5, 3, 1)


def exchange(blocks):
    return lax.all_to_all(blocks, "term", 0, 0, axis_index_groups=[list(ORDER)])


def body(wavefunction, left_ops, right_ops, term_table, coefficients, term_counts):
    count = lax.axis_size("chain")
    right = lax.ppermute(right_ops, "chain", [(s, (s - 1) % count) for s in range(count)])
    chain = lax.axis_index("chain") % 16
    own = jnp.where(chain % 2 == 0, 7000, 0)
    for bond, wait in ((0, 0), (6, 0), (7, 5000), (14, 0), (15, 3500)):
        own = jnp.where(chain == bond, wait, own)
    late = own.reshape(1, 1).astype(jnp.int32)
    shape = jax.ShapeDtypeStruct
    table, coef, left, wave = pl.pallas_call(
        stage_kernel,
        out_shape=tuple(shape(a.shape, a.dtype) for a in (term_table, coefficients, left_ops, wavefunction)),
        in_specs=[HBM] * 4,
        out_specs=(VMEM,) * 4,
        scratch_shapes=[pltpu.SemaphoreType.DMA((4,))],
        compiler_params=params(4),
        name="stage",
    )(*(pltpu.with_memory_space_constraint(a, pltpu.HBM) for a in (term_table, coefficients, left_ops, wavefunction)))
    mixed, norm = pl.pallas_call(
        first_left_kernel,
        out_shape=(shape((4, 256, 2048), BF16), shape((1, 128), F32)),
        in_specs=[SMEM, SMEM, SMEM, VMEM, VMEM],
        out_specs=(VMEM, VMEM),
        scratch_shapes=[pltpu.VMEM((32, 256, 256), F32)],
        compiler_params=params(24),
        name="first_left",
    )(table, coef, term_counts, left, wave)
    partial = pl.pallas_call(
        functools.partial(first_right_kernel, ORDER),
        out_shape=shape((16, 64, 256), BF16),
        in_specs=[SMEM, VMEM, VMEM],
        out_specs=VMEM,
        compiler_params=params(16),
        name="first_right",
    )(late, mixed, right)
    first, copies = pl.pallas_call(
        sum_kernel,
        out_shape=(shape((1, 4, 16, 256), BF16), shape((16, 64, 256), BF16)),
        in_specs=[VMEM],
        out_specs=(VMEM, VMEM),
        compiler_params=params(8),
        name="sum",
    )(exchange(partial))
    partial, scale = pl.pallas_call(
        functools.partial(second_kernel, ORDER),
        out_shape=(shape((16, 64, 256), BF16), shape((1, 128), F32)),
        in_specs=[SMEM, SMEM, SMEM, VMEM, VMEM, VMEM, VMEM, VMEM],
        out_specs=(VMEM, VMEM),
        scratch_shapes=[
            pltpu.VMEM((4, 256, 256), BF16),
            pltpu.VMEM((4, 8, 256, 256), BF16),
            pltpu.VMEM((4, 256, 256), F32),
        ],
        compiler_params=params(16),
        name="second",
    )(table, coef, term_counts, norm, exchange(copies), wave, left, right)
    second = pl.pallas_call(
        scale_kernel,
        out_shape=shape((1, 4, 16, 256), BF16),
        in_specs=[VMEM, VMEM],
        out_specs=VMEM,
        compiler_params=params(8),
        name="scale",
    )(scale, exchange(partial))
    return first, second


def solution(mesh):
    in_specs = (
        P("chain", None, None, None),
        P("chain", "term", None, None),
        P("chain", "term", None, None),
        P(None, "chain", "term"),
        P("chain", "term"),
        P("chain", "term"),
    )
    out_specs = (P("chain", None, "term", None), P("chain", None, "term", None))
    return jax.shard_map(body, mesh=mesh, in_specs=in_specs, out_specs=out_specs, check_vma=False)
```

time: 101 us -> 84.3 us (0.83)
  the two profiles are of different devices: /device:TPU:326 before, /device:TPU:2 now
where the time goes in v2:
time: 84.3 us; the launch traced here: 84 us
  blocking collectives  52.2 us (62%)
  starting transfers between devices  11.9 us (14%)
  Pallas kernels  11.6 us (14%)
  waiting for transfers between devices  6.86 us (8%)
  between operations  1.37 us (2%)
    all_to_all x3, blocking collectives, exchange(): return lax.all_to_all(blocks, 'term', 0, 0, axis_index_groups=[list(ORDER)])  52.2 us
    ppermute x1, starting transfers between devices, body(): lax.ppermute(right_ops, 'chain', [(s, (s - 1) % count) for s in range(cou...  11.9 us
    ppermute x1, waiting for transfers between devices, body(): lax.ppermute(right_ops, 'chain', [(s, (s - 1) % count) for s in range(cou...  6.86 us
    pallas_call x1, Pallas kernels, body(): pl.pallas_call(functools.partial(second_kernel, ORDER), out_shape=(shape(...  3.9 us
    pallas_call x1, Pallas kernels, body(): pl.pallas_call(first_left_kernel, out_shape=(shape((4, 256, 2048), BF16),...  3.64 us
  transfers between devices with their start and end apart: 1, of which 1 were waited for; matrix products, arithmetic and copies ran while one was open for 0% of the time, Pallas kernels for 6%

profile of v2, /device:TPU:2, one launch (start us, length us, event | category | flops | bytes accessed | tf_op | source)
XLA Modules:
  0.0 84.0 jit_solution(15340582641306208089)
XLA Ops:
  0.6 11.9 %collective-permute-start = (bf16[1,8,256,256]{3,2,1,0:T(8,128)(2,1)}, bf16[1,8,256,256]{3,2,1,0:T(8,128)(2,1)S(1)}, u32[]{:S(2)}, u32[]{:S(2)}) collective-permute-start(bf16[1,8,256,256]{3,2,1,0:T(8,128)(2,1)} %param.8), channel_id=1, source_target_pairs={{0,496},{16,0},{32,16},{48,32},{64,48},{80,64},{96,80},{112,96},{1... | collective-permute-start | bytes 3145736 | tf_op jit(solution)/shard_map/ppermute | solution.py:155
  13.3 1.4 %stage.1 = (s32[4,1,32]{2,1,0:T(1,128)S(1)}, f32[1,32]{1,0:T(1,128)S(1)}, bf16[1,8,256,256]{3,2,1,0:T(8,128)(2,1)S(1)}, bf16[1,4,256,256]{3,2,1,0:T(8,128)(2,1)S(1)}) custom-call(s32[4,1,32]{2,1,0:T(1,128)} %table_ref.1, f32[1,32]{1,0:T(1,128)} %coef_ref.1, bf16[1,8,256,256]{3,2,1,0:T(8,128)(2,1)} %left_ref.1, bf16[1,4,256,256]{3,2,1,0:T(8,128)(2,1)} %wave_ref.1), custom_call_target="tpu_custom_call" | custom-call | tf_op jit(solution)/shard_map/stage/pallas_call | solution.py:162
  14.7 3.6 %first_left.1 = (bf16[4,256,2048]{2,1,0:T(8,128)(2,1)S(1)}, f32[1,128]{1,0:T(1,128)S(1)}) custom-call(s32[4,1,32]{2,1,0:T(1,128)S(1)} %get-tuple-element.12.table_ref, f32[1,32]{1,0:T(1,128)S(1)} %get-tuple-element.13.coef_ref, s32[1,1]{1,0:T(1,128)S(6)} %copy.8.count_ref, bf16[1,8,256,256]{3,2,1,0:T(8,128)(2,1)S(1)} %get-tuple-element.14.left_ref, ...), custom_call_target="tpu_custom_call" | custom-call | tf_op jit(solution)/shard_map/first_left/pallas_call | solution.py:171
  18.3 6.9 %collective-permute-done.right_ref = bf16[1,8,256,256]{3,2,1,0:T(8,128)(2,1)S(1)} collective-permute-done((bf16[1,8,256,256]{3,2,1,0:T(8,128)(2,1)}, bf16[1,8,256,256]{3,2,1,0:T(8,128)(2,1)S(1)}, u32[]{:S(2)}, u32[]{:S(2)}) %collective-permute-start) | collective-permute-done | bytes 1048608 | tf_op jit(solution)/shard_map/ppermute | solution.py:155
  25.2 1.3 %first_right.1 = bf16[16,64,256]{2,1,0:T(8,128)(2,1)S(1)} custom-call(s32[1,1]{1,0:T(1,128)} %bitcast.late_ref, bf16[4,256,2048]{2,1,0:T(8,128)(2,1)S(1)} %get-tuple-element.16.mixed_ref, bf16[1,8,256,256]{3,2,1,0:T(8,128)(2,1)S(1)} %collective-permute-done.right_ref), custom_call_target="tpu_custom_call" | custom-call | tf_op jit(solution)/shard_map/first_right/pallas_call | solution.py:180
  26.5 20.7 %all_to_all.15.parts_ref = bf16[16,64,256]{2,1,0:T(8,128)(2,1)S(1)} all-to-all(bf16[16,64,256]{2,1,0:T(8,128)(2,1)S(1)} %first_right.1), channel_id=1, replica_groups={{0,2,4,6,8,10,12,14,15,13,11,9,7,5,3,1},{16,18,20,22,24,26,28,30,31,29,..., dimensions={0} | all-to-all | bytes 1048576 | tf_op jit(solution)/shard_map/all_to_all | solution.py:150
  47.2 0.7 sum.1
  47.9 15.6 %all_to_all.16.blocks_ref = bf16[16,64,256]{2,1,0:T(8,128)(2,1)S(1)} all-to-all(bf16[16,64,256]{2,1,0:T(8,128)(2,1)S(1)} %get-tuple-element.19), channel_id=1, replica_groups={{0,2,4,6,8,10,12,14,15,13,11,9,7,5,3,1},{16,18,20,22,24,26,28,30,31,29,..., dimensions={0} | all-to-all | bytes 1048576 | tf_op jit(solution)/shard_map/all_to_all | solution.py:150
  63.6 3.9 %second.1 = (bf16[16,64,256]{2,1,0:T(8,128)(2,1)S(1)}, f32[1,128]{1,0:T(1,128)S(1)}) custom-call(s32[4,1,32]{2,1,0:T(1,128)S(1)} %get-tuple-element.12.table_ref, f32[1,32]{1,0:T(1,128)S(1)} %get-tuple-element.13.coef_ref, s32[1,1]{1,0:T(1,128)S(6)} %copy.8.count_ref, f32[1,128]{1,0:T(1,128)S(1)} %get-tuple-element.18.norm_ref, ...), custom_call_target="tpu_custom_call" | custom-call | tf_op jit(solution)/shard_map/second/pallas_call | solution.py:196
  67.5 15.8 %all_to_all.17.parts_ref = bf16[16,64,256]{2,1,0:T(8,128)(2,1)S(1)} all-to-all(bf16[16,64,256]{2,1,0:T(8,128)(2,1)S(1)} %get-tuple-element.21), channel_id=1, replica_groups={{0,2,4,6,8,10,12,14,15,13,11,9,7,5,3,1},{16,18,20,22,24,26,28,30,31,29,..., dimensions={0} | all-to-all | bytes 1048576 | tf_op jit(solution)/shard_map/all_to_all | solution.py:150
  83.3 0.7 scale.1
Async XLA Ops:
  0.6 24.6 %collective-permute-start = (bf16[1,8,256,256]{3,2,1,0:T(8,128)(2,1)}, bf16[1,8,256,256]{3,2,1,0:T(8,128)(2,1)S(1)}, u32[]{:S(2)}, u32[]{:S(2)}) collective-permute-start(bf16[1,8,256,256]{3,2,1,0:T(8,128)(2,1)} %param.8), channel_id=1, source_target_pairs={{0,496},{16,0},{32,16},{48,32},{64,48},{80,64},{96,80},{112,96},{1... | collective-permute-start | bytes 3145736 | tf_op jit(solution)/shard_map/ppermute | solution.py:155

commit v3 on v2

--- a/solution.py
+++ b/solution.py
@@ -16,10 +16,11 @@
 
 
 def left_products(left_ref, vector, product_ref):
-    left = left_ref[0].reshape(8 * 256, 256)
     for src in range(4):
-        product = jnp.dot(left, vector(src), preferred_element_type=F32)
-        product_ref[src] = product.astype(BF16).reshape(8, 256, 256)
+        for half in range(0, 8, 2):
+            left = left_ref[0, pl.ds(half, 2)].reshape(512, 256)
+            product = jnp.dot(left, vector(src), preferred_element_type=F32)
+            product_ref[src, pl.ds(half, 2)] = product.astype(BF16).reshape(2, 256, 256)
 
 
 def right_sums(table_ref, coef_ref, count_ref, product_ref, right_ref, total_ref):
@@ -34,7 +35,7 @@
         total_ref[dst] = total_ref[dst] + weight * outer
         return 0
 
-    lax.fori_loop(0, 32, step, 0, unroll=16)
+    lax.fori_loop(0, 32, step, 0, unroll=32)
 
 
 def stage_kernel(table_ref, coef_ref, left_ref, wave_ref, table_out, coef_out, left_out, wave_out, sems):
@@ -83,12 +84,11 @@
             out_ref[place, pl.ds(16 * k, 16), :] = total[16 * owner : 16 * owner + 16].astype(BF16)
 
 
-def sum_kernel(parts_ref, first_ref, copies_ref):
+def sum_kernel(parts_ref, copies_ref):
     rows = parts_ref[0].astype(F32)
     for part in range(1, 16):
         rows = rows + parts_ref[part].astype(F32)
     first = rows.astype(BF16)
-    first_ref[0] = first.reshape(4, 16, 256)
     for copy in range(16):
         copies_ref[copy] = first
 
@@ -131,7 +131,8 @@
     scale_ref[...] = lax.rsqrt(jnp.full((1, 128), jnp.sum(square) / entries + epsilon, F32))
 
 
-def scale_kernel(scale_ref, parts_ref, out_ref):
+def scale_kernel(scale_ref, first_ref, parts_ref, first_out, out_ref):
+    first_out[0] = first_ref[0].reshape(4, 16, 256)
     rows = parts_ref[0].astype(F32)
     for part in range(1, 16):
         rows = rows + parts_ref[part].astype(F32)
@@ -185,11 +186,11 @@
         compiler_params=params(16),
         name="first_right",
     )(late, mixed, right)
-    first, copies = pl.pallas_call(
+    copies = pl.pallas_call(
         sum_kernel,
-        out_shape=(shape((1, 4, 16, 256), BF16), shape((16, 64, 256), BF16)),
+        out_shape=shape((16, 64, 256), BF16),
         in_specs=[VMEM],
-        out_specs=(VMEM, VMEM),
+        out_specs=VMEM,
         compiler_params=params(8),
         name="sum",
     )(exchange(partial))
@@ -206,15 +207,14 @@
         compiler_params=params(16),
         name="second",
     )(table, coef, term_counts, norm, exchange(copies), wave, left, right)
-    second = pl.pallas_call(
+    return pl.pallas_call(
         scale_kernel,
-        out_shape=shape((1, 4, 16, 256), BF16),
-        in_specs=[VMEM, VMEM],
-        out_specs=VMEM,
+        out_shape=(shape((1, 4, 16, 256), BF16), shape((1, 4, 16, 256), BF16)),
+        in_specs=[VMEM, VMEM, VMEM],
+        out_specs=(VMEM, VMEM),
         compiler_params=params(8),
         name="scale",
-    )(scale, exchange(partial))
-    return first, second
+    )(scale, copies, exchange(partial))
 
 
 def solution(mesh):

time: 84.3 us -> 83.4 us (0.989)
  Pallas kernels: 11.6 us -> 10.7 us
where the time goes in v3:
time: 83.4 us; the launch traced here: 83.2 us
  blocking collectives  52.2 us (63%)
  starting transfers between devices  11.9 us (14%)
  Pallas kernels  10.7 us (13%)
  waiting for transfers between devices  6.86 us (8%)
  between operations  1.38 us (2%)
    all_to_all x3, blocking collectives, exchange(): return lax.all_to_all(blocks, 'term', 0, 0, axis_index_groups=[list(ORDER)])  52.2 us
    ppermute x1, starting transfers between devices, body(): lax.ppermute(right_ops, 'chain', [(s, (s - 1) % count) for s in range(cou...  11.9 us
    ppermute x1, waiting for transfers between devices, body(): lax.ppermute(right_ops, 'chain', [(s, (s - 1) % count) for s in range(cou...  6.86 us
    pallas_call x1, Pallas kernels, body(): pl.pallas_call(functools.partial(second_kernel, ORDER), out_shape=(shape(...  3.65 us
    pallas_call x1, Pallas kernels, body(): pl.pallas_call(first_left_kernel, out_shape=(shape((4, 256, 2048), BF16),...  3.64 us
  transfers between devices with their start and end apart: 1, of which 1 were waited for; matrix products, arithmetic and copies ran while one was open for 0% of the time, Pallas kernels for 6%

profile of v3, /device:TPU:2, one launch (start us, length us, event | category | flops | bytes accessed | tf_op | source)
XLA Modules:
  0.0 83.2 jit_solution(13147022135712761024)
XLA Ops:
  0.6 11.9 %collective-permute-start = (bf16[1,8,256,256]{3,2,1,0:T(8,128)(2,1)}, bf16[1,8,256,256]{3,2,1,0:T(8,128)(2,1)S(1)}, u32[]{:S(2)}, u32[]{:S(2)}) collective-permute-start(bf16[1,8,256,256]{3,2,1,0:T(8,128)(2,1)} %param.8), channel_id=1, source_target_pairs={{0,496},{16,0},{32,16},{48,32},{64,48},{80,64},{96,80},{112,96},{1... | collective-permute-start | bytes 3145736 | tf_op jit(solution)/shard_map/ppermute | solution.py:156
  13.3 1.4 %stage.1 = (s32[4,1,32]{2,1,0:T(1,128)S(1)}, f32[1,32]{1,0:T(1,128)S(1)}, bf16[1,8,256,256]{3,2,1,0:T(8,128)(2,1)S(1)}, bf16[1,4,256,256]{3,2,1,0:T(8,128)(2,1)S(1)}) custom-call(s32[4,1,32]{2,1,0:T(1,128)} %table_ref.1, f32[1,32]{1,0:T(1,128)} %coef_ref.1, bf16[1,8,256,256]{3,2,1,0:T(8,128)(2,1)} %left_ref.1, bf16[1,4,256,256]{3,2,1,0:T(8,128)(2,1)} %wave_ref.1), custom_call_target="tpu_custom_call" | custom-call | tf_op jit(solution)/shard_map/stage/pallas_call | solution.py:163
  14.7 3.6 %first_left.1 = (bf16[4,256,2048]{2,1,0:T(8,128)(2,1)S(1)}, f32[1,128]{1,0:T(1,128)S(1)}) custom-call(s32[4,1,32]{2,1,0:T(1,128)S(1)} %get-tuple-element.10.table_ref, f32[1,32]{1,0:T(1,128)S(1)} %get-tuple-element.11.coef_ref, s32[1,1]{1,0:T(1,128)S(6)} %copy.8.count_ref, bf16[1,8,256,256]{3,2,1,0:T(8,128)(2,1)S(1)} %get-tuple-element.12.left_ref, ...), custom_call_target="tpu_custom_call" | custom-call | tf_op jit(solution)/shard_map/first_left/pallas_call | solution.py:172
  18.3 6.9 %collective-permute-done.right_ref = bf16[1,8,256,256]{3,2,1,0:T(8,128)(2,1)S(1)} collective-permute-done((bf16[1,8,256,256]{3,2,1,0:T(8,128)(2,1)}, bf16[1,8,256,256]{3,2,1,0:T(8,128)(2,1)S(1)}, u32[]{:S(2)}, u32[]{:S(2)}) %collective-permute-start) | collective-permute-done | bytes 1048608 | tf_op jit(solution)/shard_map/ppermute | solution.py:156
  25.2 1.3 %first_right.1 = bf16[16,64,256]{2,1,0:T(8,128)(2,1)S(1)} custom-call(s32[1,1]{1,0:T(1,128)} %bitcast.late_ref, bf16[4,256,2048]{2,1,0:T(8,128)(2,1)S(1)} %get-tuple-element.15.mixed_ref, bf16[1,8,256,256]{3,2,1,0:T(8,128)(2,1)S(1)} %collective-permute-done.right_ref), custom_call_target="tpu_custom_call" | custom-call | tf_op jit(solution)/shard_map/first_right/pallas_call | solution.py:181
  26.5 20.8 %all_to_all.15.parts_ref = bf16[16,64,256]{2,1,0:T(8,128)(2,1)S(1)} all-to-all(bf16[16,64,256]{2,1,0:T(8,128)(2,1)S(1)} %first_right.1), channel_id=1, replica_groups={{0,2,4,6,8,10,12,14,15,13,11,9,7,5,3,1},{16,18,20,22,24,26,28,30,31,29,..., dimensions={0} | all-to-all | bytes 1048576 | tf_op jit(solution)/shard_map/all_to_all | solution.py:151
  47.3 0.1 sum.1.first_ref
  47.4 15.6 %all_to_all.16.blocks_ref = bf16[16,64,256]{2,1,0:T(8,128)(2,1)S(1)} all-to-all(bf16[16,64,256]{2,1,0:T(8,128)(2,1)S(1)} %sum.1.first_ref), channel_id=1, replica_groups={{0,2,4,6,8,10,12,14,15,13,11,9,7,5,3,1},{16,18,20,22,24,26,28,30,31,29,..., dimensions={0} | all-to-all | bytes 1048576 | tf_op jit(solution)/shard_map/all_to_all | solution.py:151
  63.0 3.7 %second.1 = (bf16[16,64,256]{2,1,0:T(8,128)(2,1)S(1)}, f32[1,128]{1,0:T(1,128)S(1)}) custom-call(s32[4,1,32]{2,1,0:T(1,128)S(1)} %get-tuple-element.10.table_ref, f32[1,32]{1,0:T(1,128)S(1)} %get-tuple-element.11.coef_ref, s32[1,1]{1,0:T(1,128)S(6)} %copy.8.count_ref, f32[1,128]{1,0:T(1,128)S(1)} %get-tuple-element.14.norm_ref, ...), custom_call_target="tpu_custom_call" | custom-call | tf_op jit(solution)/shard_map/second/pallas_call | solution.py:197
  66.6 15.8 %all_to_all.17.parts_ref = bf16[16,64,256]{2,1,0:T(8,128)(2,1)S(1)} all-to-all(bf16[16,64,256]{2,1,0:T(8,128)(2,1)S(1)} %get-tuple-element.17), channel_id=1, replica_groups={{0,2,4,6,8,10,12,14,15,13,11,9,7,5,3,1},{16,18,20,22,24,26,28,30,31,29,..., dimensions={0} | all-to-all | bytes 1048576 | tf_op jit(solution)/shard_map/all_to_all | solution.py:151
  82.5 0.7 scale.1
Async XLA Ops:
  0.6 24.6 %collective-permute-start = (bf16[1,8,256,256]{3,2,1,0:T(8,128)(2,1)}, bf16[1,8,256,256]{3,2,1,0:T(8,128)(2,1)S(1)}, u32[]{:S(2)}, u32[]{:S(2)}) collective-permute-start(bf16[1,8,256,256]{3,2,1,0:T(8,128)(2,1)} %param.8), channel_id=1, source_target_pairs={{0,496},{16,0},{32,16},{48,32},{64,48},{80,64},{96,80},{112,96},{1... | collective-permute-start | bytes 3145736 | tf_op jit(solution)/shard_map/ppermute | solution.py:156

commit v4 on v3

--- a/solution.py
+++ b/solution.py
@@ -78,10 +78,13 @@
     pl.delay(late_ref[0, 0])
 
     right = right_ref[0].reshape(8 * 256, 256)
-    for k in range(4):
-        total = jnp.dot(mixed_ref[k], right, preferred_element_type=F32)
-        for place, owner in enumerate(order):
-            out_ref[place, pl.ds(16 * k, 16), :] = total[16 * owner : 16 * owner + 16].astype(BF16)
+    for pair in range(0, 4, 2):
+        mixed = mixed_ref[pl.ds(pair, 2)].reshape(2 * 256, 8 * 256)
+        total = jnp.dot(mixed, right, preferred_element_type=F32)
+        for k in range(2):
+            for place, owner in enumerate(order):
+                rows = total[256 * k + 16 * owner : 256 * k + 16 * owner + 16]
+                out_ref[place, pl.ds(16 * (pair + k), 16), :] = rows.astype(BF16)
 
 
 def sum_kernel(parts_ref, copies_ref):
@@ -144,7 +147,7 @@
     return pltpu.CompilerParams(vmem_limit_bytes=mib << 20)
 
 
-ORDER = (0, 2, 4, 6, 8, 10, 12, 14, 15, 13, 11, 9, 7, 5, 3, 1)
+ORDER = (0, 1, 3, 2, 4, 5, 7, 6, 8, 9, 11, 10, 12, 13, 15, 14)
 
 
 def exchange(blocks):

time: 83.4 us -> 83 us (level)
  no operation moved by 1% of the time
where the time goes in v4:
time: 83 us; the launch traced here: 82.7 us
  blocking collectives  51.8 us (62%)
  starting transfers between devices  11.9 us (14%)
  Pallas kernels  10.7 us (13%)
  waiting for transfers between devices  6.86 us (8%)
  between operations  1.37 us (2%)
    all_to_all x3, blocking collectives, exchange(): return lax.all_to_all(blocks, 'term', 0, 0, axis_index_groups=[list(ORDER)])  51.8 us
    ppermute x1, starting transfers between devices, body(): lax.ppermute(right_ops, 'chain', [(s, (s - 1) % count) for s in range(cou...  11.9 us
    ppermute x1, waiting for transfers between devices, body(): lax.ppermute(right_ops, 'chain', [(s, (s - 1) % count) for s in range(cou...  6.86 us
    pallas_call x1, Pallas kernels, body(): pl.pallas_call(functools.partial(second_kernel, ORDER), out_shape=(shape(...  3.68 us
    pallas_call x1, Pallas kernels, body(): pl.pallas_call(first_left_kernel, out_shape=(shape((4, 256, 2048), BF16),...  3.64 us
  transfers between devices with their start and end apart: 1, of which 1 were waited for; matrix products, arithmetic and copies ran while one was open for 0% of the time, Pallas kernels for 6%

profile of v4, /device:TPU:2, one launch (start us, length us, event | category | flops | bytes accessed | tf_op | source)
XLA Modules:
  0.0 82.7 jit_solution(9816354877695576725)
XLA Ops:
  0.6 11.9 %collective-permute-start = (bf16[1,8,256,256]{3,2,1,0:T(8,128)(2,1)}, bf16[1,8,256,256]{3,2,1,0:T(8,128)(2,1)S(1)}, u32[]{:S(2)}, u32[]{:S(2)}) collective-permute-start(bf16[1,8,256,256]{3,2,1,0:T(8,128)(2,1)} %param.8), channel_id=1, source_target_pairs={{0,496},{16,0},{32,16},{48,32},{64,48},{80,64},{96,80},{112,96},{1... | collective-permute-start | bytes 3145736 | tf_op jit(solution)/shard_map/ppermute | solution.py:159
  13.3 1.4 %stage.1 = (s32[4,1,32]{2,1,0:T(1,128)S(1)}, f32[1,32]{1,0:T(1,128)S(1)}, bf16[1,8,256,256]{3,2,1,0:T(8,128)(2,1)S(1)}, bf16[1,4,256,256]{3,2,1,0:T(8,128)(2,1)S(1)}) custom-call(s32[4,1,32]{2,1,0:T(1,128)} %table_ref.1, f32[1,32]{1,0:T(1,128)} %coef_ref.1, bf16[1,8,256,256]{3,2,1,0:T(8,128)(2,1)} %left_ref.1, bf16[1,4,256,256]{3,2,1,0:T(8,128)(2,1)} %wave_ref.1), custom_call_target="tpu_custom_call" | custom-call | tf_op jit(solution)/shard_map/stage/pallas_call | solution.py:166
  14.7 3.6 %first_left.1 = (bf16[4,256,2048]{2,1,0:T(8,128)(2,1)S(1)}, f32[1,128]{1,0:T(1,128)S(1)}) custom-call(s32[4,1,32]{2,1,0:T(1,128)S(1)} %get-tuple-element.10.table_ref, f32[1,32]{1,0:T(1,128)S(1)} %get-tuple-element.11.coef_ref, s32[1,1]{1,0:T(1,128)S(6)} %copy.8.count_ref, bf16[1,8,256,256]{3,2,1,0:T(8,128)(2,1)S(1)} %get-tuple-element.12.left_ref, ...), custom_call_target="tpu_custom_call" | custom-call | tf_op jit(solution)/shard_map/first_left/pallas_call | solution.py:175
  18.3 6.9 %collective-permute-done.right_ref = bf16[1,8,256,256]{3,2,1,0:T(8,128)(2,1)S(1)} collective-permute-done((bf16[1,8,256,256]{3,2,1,0:T(8,128)(2,1)}, bf16[1,8,256,256]{3,2,1,0:T(8,128)(2,1)S(1)}, u32[]{:S(2)}, u32[]{:S(2)}) %collective-permute-start) | collective-permute-done | bytes 1048608 | tf_op jit(solution)/shard_map/ppermute | solution.py:159
  25.2 1.2 %first_right.1 = bf16[16,64,256]{2,1,0:T(8,128)(2,1)S(1)} custom-call(s32[1,1]{1,0:T(1,128)} %bitcast.late_ref, bf16[4,256,2048]{2,1,0:T(8,128)(2,1)S(1)} %get-tuple-element.15.mixed_ref, bf16[1,8,256,256]{3,2,1,0:T(8,128)(2,1)S(1)} %collective-permute-done.right_ref), custom_call_target="tpu_custom_call" | custom-call | tf_op jit(solution)/shard_map/first_right/pallas_call | solution.py:184
  26.4 20.0 %all_to_all.15.parts_ref = bf16[16,64,256]{2,1,0:T(8,128)(2,1)S(1)} all-to-all(bf16[16,64,256]{2,1,0:T(8,128)(2,1)S(1)} %first_right.1), channel_id=1, replica_groups={{0,1,3,2,4,5,7,6,8,9,11,10,12,13,15,14},{16,17,19,18,20,21,23,22,24,25,..., dimensions={0} | all-to-all | bytes 1048576 | tf_op jit(solution)/shard_map/all_to_all | solution.py:154
  46.4 0.1 sum.1.first_ref
  46.5 16.0 %all_to_all.16.blocks_ref = bf16[16,64,256]{2,1,0:T(8,128)(2,1)S(1)} all-to-all(bf16[16,64,256]{2,1,0:T(8,128)(2,1)S(1)} %sum.1.first_ref), channel_id=1, replica_groups={{0,1,3,2,4,5,7,6,8,9,11,10,12,13,15,14},{16,17,19,18,20,21,23,22,24,25,..., dimensions={0} | all-to-all | bytes 1048576 | tf_op jit(solution)/shard_map/all_to_all | solution.py:154
  62.5 3.7 %second.1 = (bf16[16,64,256]{2,1,0:T(8,128)(2,1)S(1)}, f32[1,128]{1,0:T(1,128)S(1)}) custom-call(s32[4,1,32]{2,1,0:T(1,128)S(1)} %get-tuple-element.10.table_ref, f32[1,32]{1,0:T(1,128)S(1)} %get-tuple-element.11.coef_ref, s32[1,1]{1,0:T(1,128)S(6)} %copy.8.count_ref, f32[1,128]{1,0:T(1,128)S(1)} %get-tuple-element.14.norm_ref, ...), custom_call_target="tpu_custom_call" | custom-call | tf_op jit(solution)/shard_map/second/pallas_call | solution.py:200
  66.2 15.8 %all_to_all.17.parts_ref = bf16[16,64,256]{2,1,0:T(8,128)(2,1)S(1)} all-to-all(bf16[16,64,256]{2,1,0:T(8,128)(2,1)S(1)} %get-tuple-element.17), channel_id=1, replica_groups={{0,1,3,2,4,5,7,6,8,9,11,10,12,13,15,14},{16,17,19,18,20,21,23,22,24,25,..., dimensions={0} | all-to-all | bytes 1048576 | tf_op jit(solution)/shard_map/all_to_all | solution.py:154
  82.0 0.7 scale.1
Async XLA Ops:
  0.6 24.6 %collective-permute-start = (bf16[1,8,256,256]{3,2,1,0:T(8,128)(2,1)}, bf16[1,8,256,256]{3,2,1,0:T(8,128)(2,1)S(1)}, u32[]{:S(2)}, u32[]{:S(2)}) collective-permute-start(bf16[1,8,256,256]{3,2,1,0:T(8,128)(2,1)} %param.8), channel_id=1, source_target_pairs={{0,496},{16,0},{32,16},{48,32},{64,48},{80,64},{96,80},{112,96},{1... | collective-permute-start | bytes 3145736 | tf_op jit(solution)/shard_map/ppermute | solution.py:159
